TPU v7x, 128 devices: a whole 4x4x4 slice. The times are simulated.
128 devices in a mesh: img: 8 (over x, core), pos: 16 (over z, y).
Axes of the slice: x: 4, y: 4, z: 4, core: 2. Of those that a mesh axis runs over, the one named last changes fastest.
Arguments:
- features: bfloat16 [16384, 32, 1536], P(('img', 'pos')), may hold values from -6 to 6
- channel_index: int32 [550], replicated, may hold values from 0 to 1535, as said below
- image_counts: int32 [128], P(('img', 'pos')), may hold values from 32 to 128, as said below
Outputs:
- centres: float32 [32, 550], P('pos')
- covars: float32 [32, 550, 550], P('pos')
Inputs may be any that keep to these rules, and one draw needn't show every extreme that they name: `channel_index`: distinct channel numbers. `image_counts`: some device uses all 128 slots and some only a quarter.
All inputs are finite; a program needn't handle non-finite values.
Results may differ from a plain program's by a relative error of at most 0.0003.
Values may be sent and summed in bfloat16 or wider, within the bound.
A program may use at most 128 MiB of HBM per device.

v0:
```python
import jax
import jax.numpy as jnp
from jax import lax
from jax.sharding import PartitionSpec as P

REG = 0.01


def combined_all(value, axis, combine):
    everything = jax.tree.map(lambda part: lax.all_gather(part, axis), value)
    initial = jax.tree.map(lambda part: part[0], everything)

    def lap(k, so_far):
        return combine(so_far, jax.tree.map(lambda part: part[k], everything))

    return lax.fori_loop(1, lax.axis_size(axis), lap, initial)


def moments(received):
    rows = received[:, 0]
    sq_sum = jnp.einsum("ipk,ipl->pkl", rows, rows, preferred_element_type=jnp.float32)
    lin_sum = jnp.sum(rows.astype(jnp.float32), axis=0)
    return (sq_sum, lin_sum)


def body(features, channel_index, image_counts):
    slots = features.shape[0]
    owners = lax.axis_size("pos")
    owned = features.shape[1] // owners
    usable = lax.iota(jnp.int32, slots) < image_counts[0]
    masked = features * usable.astype(jnp.bfloat16)[:, None, None]
    chosen = jnp.take(masked, channel_index, axis=2)
    chosen = chosen.reshape(slots, owners, owned, chosen.shape[2])
    sq_sum, lin_sum = moments(
        lax.all_to_all(chosen, "pos", split_axis=1, concat_axis=0, tiled=True)
    )
    group_total = lax.psum(image_counts.astype(jnp.float32)[0], "pos")
    width = channel_index.shape[0]
    identity_mat = jnp.eye(width, dtype=jnp.float32)
    centre = lin_sum / group_total
    scatter_mat = sq_sum - group_total * centre[:, :, None] * centre[:, None, :]

    def combine(earlier, later):
        count_low, centre_low, scatter_low = earlier
        count_high, centre_high, scatter_high = later
        joined = count_low + count_high
        offset = centre_high - centre_low
        new_centre = centre_low + offset * (count_high / joined)
        weight_pair = count_low * count_high / joined
        new_scatter = (
            scatter_low + scatter_high + weight_pair * offset[:, :, None] * offset[:, None, :]
        )
        return (joined, new_centre, new_scatter)

    total_count, centre, scatter_mat = combined_all(
        (group_total, centre, scatter_mat), "img", combine
    )
    covar = scatter_mat / (total_count - 1.0) + REG * identity_mat
    return (centre, covar)


def solution(mesh):
    placed = (P(("img", "pos"), None, None), P(), P(("img", "pos")))
    return jax.shard_map(
        body,
        mesh=mesh,
        in_specs=placed,
        out_specs=(P("pos", None), P("pos", None, None)),
        check_vma=False,
    )
```

profile of v0, /device:TPU:1, one launch (start us, length us, event | category | flops | bytes accessed | tf_op | source)
XLA Modules:
  0.0 346.5 jit_solution(6363015843126375706)
XLA Ops:
  7.2 0.7 compare_select_fusion
  7.9 0.7 compare_and_fusion
  9.2 17.9 %copy.24 = bf16[128,32,1536]{0,1,2:T(8,128)(2,1)} copy(bf16[128,32,1536]{2,1,0:T(8,128)(2,1)} %param.5) | data formatting | bytes 25165824 | tf_op args[0]
  27.2 10.4 %broadcast_multiply_fusion.1 = bf16[128,32,1536]{0,1,2:T(8,128)(2,1)} fusion(bf16[128,32,1536]{0,1,2:T(8,128)(2,1)} %copy.24, bf16[128]{0:T(256)(128)(2,1)S(1)} %compare_convert_fusion), kind=kLoop, calls=%fused_computation.7 | loop fusion | flops 6291456 | bytes 25166080 | tf_op jit(solution)/shard_map/mul | solution.py:31
  37.6 8.9 %gather_fusion = bf16[550,128,32]{1,2,0:T(8,128)(2,1)} fusion(bf16[128,32,1536]{0,1,2:T(8,128)(2,1)} %broadcast_multiply_fusion.1, s32[1024]{0:T(1024)S(1)} %pad_clamp_fusion), kind=kCustom, calls=%fused_computation | custom fusion | bytes 9013400 | tf_op jit(solution)/shard_map/jit(_take)/gather | solution.py:32
  46.5 4.0 %copy.25 = bf16[128,32,550]{0,2,1:T(8,128)(2,1)S(1)} copy(bf16[128,32,550]{0,1,2:T(8,128)(2,1)} %bitcast.35) | data formatting | bytes 9011200 | tf_op jit(solution)/shard_map/jit(_take)/gather | solution.py:32
  50.5 2.5 broadcast_select_fusion
  53.0 7.9 %copy.26 = bf16[128,16,2,550]{0,2,3,1:T(2,128)(2,1)} copy(bf16[128,16,2,550]{0,3,2,1:T(8,128)(2,1)} %broadcast_select_fusion) | data formatting | bytes 9011200 | tf_op jit(solution)/shard_map/jit(_take)/select_n | solution.py:32
  60.9 8.6 %all-to-all-start = ((bf16[128,16,2,550]{0,2,3,1:T(2,128)(2,1)}), bf16[128,16,2,550]{0,2,3,1:T(2,128)(2,1)}, u32[]{:S(2)}, u32[]{:S(2)}) async-start(bf16[128,16,2,550]{0,2,3,1:T(2,128)(2,1)} %copy.26), calls=%async_computation | async-start | bytes 9011200 | tf_op jit(solution)/shard_map/all_to_all | solution.py:35
  69.6 0.0 all-gather.5.cloned.1.call-start
  69.6 89.4 %psum.7 = f32[]{:T(128)} all-reduce(f32[]{:T(128)} %bitcast.3), channel_id=1, replica_groups=mesh['img'=8,'pos'=16] {'pos'}, use_global_device_ids=true, to_apply=%region_0.1 | all-reduce | flops 1 | bytes 8 | tf_op jit(solution)/shard_map/psum | solution.py:37
  159.0 0.0 all-to-all-done
  159.0 5.9 %convert_reduce_fusion = f32[2,550]{0,1:T(8,128)S(1)} fusion(bf16[128,16,2,550]{0,2,3,1:T(2,128)(2,1)} %all-to-all-done), kind=kLoop, calls=%fused_computation.6 | loop fusion | flops 4504500 | bytes 4510000 | tf_op jit(solution)/shard_map/reduce_sum | solution.py:22
  164.9 0.1 copy.27
  165.0 5.0 %copy.28 = bf16[16,128,1,2,550]{1,0,4,3,2:T(8,128)(2,1)} copy(bf16[16,128,1,2,550]{1,3,4,0,2:T(2,128)(2,1)} %bitcast.11) | data formatting | bytes 9011200 | tf_op jit(solution)/shard_map/all_to_all | solution.py:35
  170.0 5.0 %squeeze.52 = bf16[2048,2,550]{0,2,1:T(8,128)(2,1)} reshape(bf16[16,128,1,2,550]{1,0,4,3,2:T(8,128)(2,1)} %copy.28) | data formatting | bytes 9011200 | tf_op jit(solution)/shard_map/squeeze | solution.py:20
  175.0 0.7 broadcast_multiply_fusion.2
  175.6 8.9 %multiply_subtract_fusion = f32[2,550,550]{2,1,0:T(8,128)} fusion(bf16[2048,2,550]{0,2,1:T(8,128)(2,1)} %squeeze.52, f32[2,550]{1,0:T(2,128)S(1)} %get-tuple-element.200, f32[2,550]{1,0:T(2,128)S(1)} %get-tuple-element.199), kind=kOutput, calls=%fused_computation.9 | convolution fusion | flops 2479289856 | bytes 6934400 | tf_op jit(solution)/shard_map/ipk,ipl->pkl/dot_general | solution.py:21
  184.6 0.0 copy-start.1
  184.6 0.0 all-gather.5.cloned.1.call-update
  184.6 0.6 copy-done.1
  185.2 0.6 dynamic-slice
  185.8 1.4 dynamic-update-slice
  187.2 19.4 %all-reduce = f32[8]{0:T(128)S(1)} all-reduce(f32[8]{0:T(128)S(1)} %dynamic-update-slice), channel_id=1, replica_groups=mesh['img'=8,'pos'=16] {'img'}, use_global_device_ids=true, to_apply=%add | all-reduce | flops 8 | bytes 64
  206.6 1.3 fusion.2
  207.9 13.3 %all-gather.2 = f32[8,2,550]{2,1,0:T(2,128)S(1)} all-gather(f32[1,2,550]{2,1,0:T(2,128)S(1)} %bitcast.38), channel_id=2, replica_groups=mesh['img'=8,'pos'=16] {'img'}, dimensions={0}, use_global_device_ids=true | all-gather | bytes 39600 | tf_op jit(solution)/shard_map/all_gather | solution.py:10
  221.2 76.9 %all-gather.5.cloned.1.call-done = f32[16,550,550]{2,1,0:T(8,128)} async-done(((f32[2,550,550]{2,1,0:T(8,128)}), f32[16,550,550]{2,1,0:T(8,128)}) %all-gather.5.cloned.1.call-update) | async-done | bytes 19360016 | tf_op jit(solution)/shard_map/all_gather | solution.py:10
  298.1 2.0 slice.18
  300.0 33.8 %while.19 = (s32[]{:T(128)}, f32[]{:T(128)}, f32[2,550]{1,0:T(2,128)S(1)}, f32[2,550,550]{2,1,0:T(8,128)S(1)}, f32[8]{0:T(128)S(1)}, /*index=5*/f32[8,2,550]{2,1...) while((s32[]{:T(128)}, f32[]{:T(128)}, f32[2,550]{1,0:T(2,128)S(1)}, ...), condition=%wide.region_3.4_spmd, body=%wide.region_2.3_spmd.sunk | while | flops 1819409 | bytes 7299827 | solution.py:16
  300.1 0.6 dynamic_slice.36
  302.4 2.5 fusion.6
  304.9 0.6 dynamic_slice.36
  307.2 2.5 fusion.6
  309.7 0.6 dynamic_slice.36
  312.1 2.5 fusion.6
  314.5 0.6 dynamic_slice.36
  316.9 2.5 fusion.6
  319.4 0.6 dynamic_slice.36
  321.7 2.5 fusion.6
  324.2 0.6 dynamic_slice.36
  326.5 2.5 fusion.6
  329.0 0.6 dynamic_slice.36
  331.4 2.5 fusion.6
  333.8 0.0 copy-start
  333.9 5.8 %fusion.1 = f32[2,550,550]{2,0,1:T(2,128)} fusion(f32[2,550,550]{2,1,0:T(8,128)S(1)} %get-tuple-element.181, f32[550,550]{1,0:T(8,128)} %fusion.2, f32[]{:T(128)S(6)} %sub.17), kind=kLoop, calls=%fused_computation.11 | loop fusion | flops 1210000 | bytes 6050004 | tf_op jit(solution)/shard_map/add | solution.py:58
  339.6 0.0 copy-done
  (18 shorter events, 0.2 us)
Async XLA Ops:
  60.9 98.1 %all-to-all-start = ((bf16[128,16,2,550]{0,2,3,1:T(2,128)(2,1)}), bf16[128,16,2,550]{0,2,3,1:T(2,128)(2,1)}, u32[]{:S(2)}, u32[]{:S(2)}) async-start(bf16[128,16,2,550]{0,2,3,1:T(2,128)(2,1)} %copy.26), calls=%async_computation | async-start | bytes 9011200 | tf_op jit(solution)/shard_map/all_to_all | solution.py:35
  69.6 228.5 %all-gather.5.cloned.1.call-start = ((), (), s32[]{:S(2)}) async-start(), calls=%async_computation.1 | async-start | bytes 25436160 | tf_op jit(solution)/shard_map/all_gather | solution.py:10
  184.6 0.7 copy-start.1
  333.8 5.8 %copy-start = (f32[2,550]{1,0:T(2,128)}, f32[2,550]{1,0:T(2,128)S(1)}, u32[]{:S(2)}) copy-start(f32[2,550]{1,0:T(2,128)S(1)} %get-tuple-element.178) | copy-start | bytes 13204
Sparse Core Ops, SparseCore 0:
  184.7 113.2 all-gather.4
where the time goes:
time: 348 us; the launch traced here: 346 us
  blocking collectives  122 us (35%)
  waiting for transfers between devices  76.9 us (22%)
  local copies, waits for them, and re-layouts  57.5 us (17%)
  other arithmetic  45.2 us (13%)
  between operations  14.8 us (4%)
  loops' own time  12.4 us (4%)
  matrix products  8.93 us (3%)
  starting transfers between devices  8.68 us (2%)
    psum x1, blocking collectives, body(): group_total = lax.psum(image_counts.astype(jnp.float32)[0], 'pos')  89.4 us
    all_gather x1, waiting for transfers between devices, combined_all(): everything = jax.tree.map(lambda part: lax.all_gather(part, axis), value)  76.9 us
    unnamed x8, local copies, waits for them, and re-layouts  20.6 us
    unnamed x1, blocking collectives  19.4 us
    add x7, other arithmetic, combine(): scatter_low + scatter_high  17.2 us
    all_gather x1, blocking collectives, combined_all(): everything = jax.tree.map(lambda part: lax.all_gather(part, axis), value)  13.3 us
    gather x2, local copies, waits for them, and re-layouts, body(): chosen = jnp.take(masked, channel_index, axis=2)  13 us
    another operation x1, loops' own time, combined_all(): return lax.fori_loop(1, lax.axis_size(axis), lap, initial)  12.4 us
  transfers between devices with their start and end apart: 2, of which 1 were waited for; matrix products, arithmetic and copies ran while one was open for 1% of the time, Pallas kernels for 0%

commit v1 on v0

--- a/solution.py
+++ b/solution.py
@@ -34,7 +34,7 @@
     sq_sum, lin_sum = moments(
         lax.all_to_all(chosen, "pos", split_axis=1, concat_axis=0, tiled=True)
     )
-    group_total = lax.psum(image_counts.astype(jnp.float32)[0], "pos")
+    group_total = jnp.sum(lax.all_gather(image_counts.astype(jnp.float32)[0], "pos"), axis=0)
     width = channel_index.shape[0]
     identity_mat = jnp.eye(width, dtype=jnp.float32)
     centre = lin_sum / group_total

time: 348 us -> 350 us (level)
    psum x1 -> x0, blocking collectives: 89.4 us -> none  [body(): group_total = lax.psum(image_counts.astype(jnp.float32)[0], 'pos')]
    unnamed x1 -> x2, blocking collectives: 19.4 us -> 107 us
    unnamed x8 -> x12, local copies, waits for them, and re-layouts: 20.6 us -> 21.2 us
where the time goes in v1:
time: 350 us; the launch traced here: 348 us
  blocking collectives  120 us (34%)
  waiting for transfers between devices  76.9 us (22%)
  local copies, waits for them, and re-layouts  58.3 us (17%)
  other arithmetic  46.6 us (13%)
  between operations  14.8 us (4%)
  loops' own time  13.7 us (4%)
  matrix products  8.94 us (3%)
  starting transfers between devices  8.82 us (3%)
    unnamed x2, blocking collectives  107 us
    all_gather x1, waiting for transfers between devices, combined_all(): everything = jax.tree.map(lambda part: lax.all_gather(part, axis), value)  76.9 us
    unnamed x12, local copies, waits for them, and re-layouts  21.2 us
    add x7, other arithmetic, combine(): scatter_low + scatter_high  17.2 us
    another operation x1, loops' own time, combined_all(): return lax.fori_loop(1, lax.axis_size(axis), lap, initial)  13.7 us
    all_gather x1, blocking collectives, combined_all(): everything = jax.tree.map(lambda part: lax.all_gather(part, axis), value)  13.3 us
    gather x2, local copies, waits for them, and re-layouts, body(): chosen = jnp.take(masked, channel_index, axis=2)  13 us
    mul x1, other arithmetic, body(): masked = features * usable.astype(jnp.bfloat16)[:, None, None]  10.4 us
  transfers between devices with their start and end apart: 2, of which 1 were waited for; matrix products, arithmetic and copies ran while one was open for 1% of the time, Pallas kernels for 0%

profile of v1, /device:TPU:1, one launch (start us, length us, event | category | flops | bytes accessed | tf_op | source)
XLA Modules:
  0.0 348.2 jit_solution(329749366503837087)
XLA Ops:
  7.2 0.7 compare_select_fusion
  7.9 0.7 compare_and_fusion
  9.2 17.9 %copy.24 = bf16[128,32,1536]{0,1,2:T(8,128)(2,1)} copy(bf16[128,32,1536]{2,1,0:T(8,128)(2,1)} %param.5) | data formatting | bytes 25165824 | tf_op args[0]
  27.2 10.4 %broadcast_multiply_fusion.1 = bf16[128,32,1536]{0,1,2:T(8,128)(2,1)} fusion(bf16[128,32,1536]{0,1,2:T(8,128)(2,1)} %copy.24, bf16[128]{0:T(256)(128)(2,1)S(1)} %compare_convert_fusion), kind=kLoop, calls=%fused_computation.7 | loop fusion | flops 6291456 | bytes 25166080 | tf_op jit(solution)/shard_map/mul | solution.py:31
  37.6 9.0 %gather_fusion = bf16[550,128,32]{1,2,0:T(8,128)(2,1)} fusion(bf16[128,32,1536]{0,1,2:T(8,128)(2,1)} %broadcast_multiply_fusion.1, s32[1024]{0:T(1024)S(1)} %pad_clamp_fusion), kind=kCustom, calls=%fused_computation | custom fusion | bytes 9013400 | tf_op jit(solution)/shard_map/jit(_take)/gather | solution.py:32
  46.5 4.0 %copy.25 = bf16[128,32,550]{0,2,1:T(8,128)(2,1)S(1)} copy(bf16[128,32,550]{0,1,2:T(8,128)(2,1)} %bitcast.35) | data formatting | bytes 9011200 | tf_op jit(solution)/shard_map/jit(_take)/gather | solution.py:32
  50.6 2.5 broadcast_select_fusion
  53.1 7.9 %copy.26 = bf16[128,16,2,550]{0,2,3,1:T(2,128)(2,1)} copy(bf16[128,16,2,550]{0,3,2,1:T(8,128)(2,1)} %broadcast_select_fusion) | data formatting | bytes 9011200 | tf_op jit(solution)/shard_map/jit(_take)/select_n | solution.py:32
  60.9 0.0 copy-start.2
  60.9 8.8 %all-to-all-start = ((bf16[128,16,2,550]{0,2,3,1:T(2,128)(2,1)}), bf16[128,16,2,550]{0,2,3,1:T(2,128)(2,1)}, u32[]{:S(2)}, u32[]{:S(2)}) async-start(bf16[128,16,2,550]{0,2,3,1:T(2,128)(2,1)} %copy.26), calls=%async_computation | async-start | bytes 9011200 | tf_op jit(solution)/shard_map/all_to_all | solution.py:35
  69.7 0.0 all-gather.5.cloned.1.call-start
  69.8 0.0 copy-done.2
  69.8 0.6 dynamic-slice
  70.4 0.7 convert_dynamic-update-slice_fusion
  71.1 87.5 %all-reduce = f32[16]{0:T(128)S(1)} all-reduce(f32[16]{0:T(128)S(1)} %convert_dynamic-update-slice_fusion), channel_id=1, replica_groups=mesh['img'=8,'pos'=16] {'pos'}, use_global_device_ids=true, to_apply=%add | all-reduce | flops 16 | bytes 128
  158.6 0.6 reduce_sum.18
  159.2 0.0 all-to-all-done
  159.2 5.9 %convert_reduce_fusion = f32[2,550]{0,1:T(8,128)S(1)} fusion(bf16[128,16,2,550]{0,2,3,1:T(2,128)(2,1)} %all-to-all-done), kind=kLoop, calls=%fused_computation.6 | loop fusion | flops 4504500 | bytes 4510000 | tf_op jit(solution)/shard_map/reduce_sum | solution.py:22
  165.2 0.1 copy.27
  165.3 5.0 %copy.28 = bf16[16,128,1,2,550]{1,0,4,3,2:T(8,128)(2,1)} copy(bf16[16,128,1,2,550]{1,3,4,0,2:T(2,128)(2,1)} %bitcast.11) | data formatting | bytes 9011200 | tf_op jit(solution)/shard_map/all_to_all | solution.py:35
  170.3 5.0 %squeeze.48 = bf16[2048,2,550]{0,2,1:T(8,128)(2,1)} reshape(bf16[16,128,1,2,550]{1,0,4,3,2:T(8,128)(2,1)} %copy.28) | data formatting | bytes 9011200 | tf_op jit(solution)/shard_map/squeeze | solution.py:20
  175.3 0.7 broadcast_multiply_fusion.2
  175.9 8.9 %multiply_subtract_fusion = f32[2,550,550]{2,1,0:T(8,128)} fusion(bf16[2048,2,550]{0,2,1:T(8,128)(2,1)} %squeeze.48, f32[2,550]{1,0:T(2,128)S(1)} %get-tuple-element.200, f32[2,550]{1,0:T(2,128)S(1)} %get-tuple-element.199), kind=kOutput, calls=%fused_computation.9 | convolution fusion | flops 2479289856 | bytes 6934400 | tf_op jit(solution)/shard_map/ipk,ipl->pkl/dot_general | solution.py:21
  184.9 0.0 copy-start.1
  184.9 0.0 all-gather.5.cloned.1.call-update
  184.9 0.6 copy-done.1
  185.5 0.6 dynamic-slice.1
  186.1 1.4 dynamic-update-slice.1
  187.5 19.4 %all-reduce.1 = f32[8]{0:T(128)S(1)} all-reduce(f32[8]{0:T(128)S(1)} %dynamic-update-slice.1), channel_id=1, replica_groups=mesh['img'=8,'pos'=16] {'img'}, use_global_device_ids=true, to_apply=%add.1 | all-reduce | flops 8 | bytes 64
  206.9 1.3 fusion.2
  208.2 13.3 %all-gather.2 = f32[8,2,550]{2,1,0:T(2,128)S(1)} all-gather(f32[1,2,550]{2,1,0:T(2,128)S(1)} %bitcast.38), channel_id=2, replica_groups=mesh['img'=8,'pos'=16] {'img'}, dimensions={0}, use_global_device_ids=true | all-gather | bytes 39600 | tf_op jit(solution)/shard_map/all_gather | solution.py:10
  221.5 76.9 %all-gather.5.cloned.1.call-done = f32[16,550,550]{2,1,0:T(8,128)} async-done(((f32[2,550,550]{2,1,0:T(8,128)}), f32[16,550,550]{2,1,0:T(8,128)}) %all-gather.5.cloned.1.call-update) | async-done | bytes 19360016 | tf_op jit(solution)/shard_map/all_gather | solution.py:10
  298.3 2.0 slice.18
  300.3 35.2 %while.19 = (s32[]{:T(128)}, f32[]{:T(128)}, f32[2,550]{1,0:T(2,128)S(1)}, f32[2,550,550]{2,1,0:T(8,128)S(1)}, f32[8]{0:T(128)S(1)}, /*index=5*/f32[8,2,550]{2,1...) while((s32[]{:T(128)}, f32[]{:T(128)}, f32[2,550]{1,0:T(2,128)S(1)}, ...), condition=%wide.region_3.4_spmd, body=%wide.region_2.3_spmd.sunk | while | flops 1819409 | bytes 7299827 | solution.py:16
  300.3 0.6 dynamic_slice.36
  302.9 2.5 fusion.6
  305.4 0.6 dynamic_slice.36
  307.9 2.5 fusion.6
  310.4 0.6 dynamic_slice.36
  313.0 2.5 fusion.6
  315.4 0.6 dynamic_slice.36
  318.0 2.5 fusion.6
  320.5 0.6 dynamic_slice.36
  323.0 2.5 fusion.6
  325.5 0.6 dynamic_slice.36
  328.1 2.5 fusion.6
  330.5 0.6 dynamic_slice.36
  333.1 2.5 fusion.6
  335.6 0.0 copy-start
  335.6 5.8 %fusion.1 = f32[2,550,550]{2,0,1:T(2,128)} fusion(f32[2,550,550]{2,1,0:T(8,128)S(1)} %get-tuple-element.181, f32[550,550]{1,0:T(8,128)} %fusion.2, f32[]{:T(128)S(6)} %sub.17), kind=kLoop, calls=%fused_computation.11 | loop fusion | flops 1210000 | bytes 6050004 | tf_op jit(solution)/shard_map/add | solution.py:58
  341.4 0.0 copy-done
  (19 shorter events, 0.2 us)
Async XLA Ops:
  60.9 8.8 %copy-start.2 = (u32[128]{0:T(128)S(1)}, u32[128]{0:T(128)}, u32[]{:S(2)}) copy-start(u32[128]{0:T(128)} %constant.64) | copy-start | bytes 1540
  60.9 98.3 %all-to-all-start = ((bf16[128,16,2,550]{0,2,3,1:T(2,128)(2,1)}), bf16[128,16,2,550]{0,2,3,1:T(2,128)(2,1)}, u32[]{:S(2)}, u32[]{:S(2)}) async-start(bf16[128,16,2,550]{0,2,3,1:T(2,128)(2,1)} %copy.26), calls=%async_computation | async-start | bytes 9011200 | tf_op jit(solution)/shard_map/all_to_all | solution.py:35
  69.7 228.6 %all-gather.5.cloned.1.call-start = ((), (), s32[]{:S(2)}) async-start(), calls=%async_computation.1 | async-start | bytes 25436160 | tf_op jit(solution)/shard_map/all_gather | solution.py:10
  184.9 0.7 copy-start.1
  335.6 5.8 %copy-start = (f32[2,550]{1,0:T(2,128)}, f32[2,550]{1,0:T(2,128)S(1)}, u32[]{:S(2)}) copy-start(f32[2,550]{1,0:T(2,128)S(1)} %get-tuple-element.178) | copy-start | bytes 13204
Sparse Core Ops, SparseCore 0:
  185.0 113.2 all-gather.4
